TPU v7x, 128 devices: a whole 4x4x4 slice. The times are simulated.
128 devices in a mesh: expert: 4 (over y), blk: 32 (over z, x, core).
Axes of the slice: x: 4, y: 4, z: 4, core: 2. Of those that a mesh axis runs over, the one named last changes fastest.
Arguments:
- tokens: bfloat16 [2, 512, 6144], P(None, 'expert', 'blk'), may hold values from -6 to 6
- expert_ids: int32 [2, 512, 2], P(None, 'expert'), may hold values from 0 to 3, all different within a row; in each aligned block of 128 rows (0 to 127, 128 to 255, ..., all dimensions but the last counted through in order) at most 128 rows name the same one
- route_share: float32 [2, 512], P(None, 'expert'), may hold values from 0.1 to 0.9
- gate_weight: bfloat16 [4, 6144, 16384], P('expert', None, 'blk'), may hold values from -0.078125 to 0.078125
- up_weight: bfloat16 [4, 6144, 16384], P('expert', None, 'blk'), may hold values from -0.078125 to 0.078125
- down_weight: bfloat16 [4, 16384, 6144], P('expert', 'blk'), may hold values from -0.09375 to 0.09375
Outputs:
- combined: bfloat16 [2, 512, 6144], P(None, 'expert', 'blk')
Inputs may be any that keep to these rules, and one draw needn't show every extreme that they name: `expert_ids`: each row names two different experts.
All inputs are finite; a program needn't handle non-finite values.
Results may differ from a plain program's by a relative error of at most 0.023.
Values may be sent and summed in bfloat16 or wider, within the bound.
No kernel may reach another device: no remote copies, remote signals or barrier semaphores. Data moves between devices by JAX's collectives and lax.ppermute only.
A program may use at most 128 MiB of HBM per device.

v0:
```python
import jax
import jax.numpy as jnp
from jax import lax
from jax.sharding import PartitionSpec as P


def routing(expert_ids, route_share, experts):
    row_count = expert_ids.shape[1]
    labels = jnp.arange(experts, dtype=jnp.int32)
    first_hit = (expert_ids[:, :, 0:1] == labels).astype(jnp.float32)
    second = (expert_ids[:, :, 1:2] == labels).astype(jnp.float32)
    chosen = first_hit + second
    weight = route_share[:, :, None] * first_hit + (1.0 - route_share[:, :, None]) * second
    slot_pos = jnp.cumsum(chosen.astype(jnp.int32), axis=1) - 1
    slot_ids = jnp.arange(row_count, dtype=jnp.int32)
    placed = ((slot_pos[:, :, :, None] == slot_ids) & (chosen[:, :, :, None] > 0)).astype(
        jnp.bfloat16
    )
    return (placed, weight)


def expert_layer(tokens, expert_ids, route_share, gate_mat, up_mat, down_mat, experts):
    step_count, row_count, feature_cols = tokens.shape
    placed, weight = routing(expert_ids, route_share, experts)
    outgoing = jnp.einsum(
        "gres,grd->gesd", placed, tokens, preferred_element_type=jnp.float32
    ).astype(jnp.bfloat16)
    arrived = lax.all_to_all(outgoing, "expert", split_axis=1, concat_axis=1, tiled=True)
    slot_rows = arrived.reshape(-1, feature_cols)
    fragment = lax.all_gather(slot_rows, "blk", axis=1, tiled=True)
    gate_pre = jnp.dot(fragment, gate_mat, preferred_element_type=jnp.float32)
    up_pre = jnp.dot(fragment, up_mat, preferred_element_type=jnp.float32)
    hidden = (jax.nn.silu(gate_pre) * up_pre).astype(jnp.bfloat16)
    summed = lax.psum_scatter(
        lax.dot_general(
            down_mat, hidden, (((0,), (1,)), ((), ())), preferred_element_type=jnp.float32
        ).astype(jnp.bfloat16),
        "blk",
        scatter_dimension=0,
        tiled=True,
    )
    returned = lax.all_to_all(
        summed.reshape(feature_cols, step_count, experts, row_count),
        "expert",
        split_axis=2,
        concat_axis=2,
        tiled=True,
    )
    picked = jnp.einsum("gres,dges->gerd", placed, returned, preferred_element_type=jnp.float32)
    combined = jnp.sum(jnp.transpose(weight, (0, 2, 1))[:, :, :, None] * picked, axis=1)
    return combined.astype(jnp.bfloat16)


def body(tokens, expert_ids, route_share, gate_weight, up_weight, down_weight):
    experts = lax.axis_size("expert")
    gate_mat = gate_weight[0]
    up_mat = up_weight[0]
    down_mat = down_weight[0]
    results = []
    for step_idx in range(tokens.shape[0]):
        results.append(
            expert_layer(
                tokens[step_idx : step_idx + 1],
                expert_ids[step_idx : step_idx + 1],
                route_share[step_idx : step_idx + 1],
                gate_mat,
                up_mat,
                down_mat,
                experts,
            )
        )
    return jnp.concatenate(results, axis=0)


def solution(mesh):
    return jax.shard_map(
        body,
        mesh=mesh,
        in_specs=(
            P(None, "expert", "blk"),
            P(None, "expert", None),
            P(None, "expert"),
            P("expert", None, "blk"),
            P("expert", None, "blk"),
            P("expert", "blk", None),
        ),
        out_specs=P(None, "expert", "blk"),
        check_vma=False,
    )
```

profile of v0, /device:TPU:0, one launch (start us, length us, event | category | flops | bytes accessed | tf_op | source)
XLA Modules:
  0.0 319.7 jit_solution(13525887074447122003)
XLA Ops:
  6.5 0.8 slice_bitcast_fusion.5
  7.3 0.1 fusion.45
  7.4 0.1 fusion.44
  7.6 0.2 reduce_window_sum.17
  7.8 0.1 copy.21
  7.8 0.1 copy.22
  7.9 1.2 fusion.26
  9.1 10.7 %all_to_all.20 = bf16[1,4,128,192]{2,3,0,1:T(8,128)(2,1)S(1)} all-to-all(bf16[1,4,128,192]{2,3,0,1:T(8,128)(2,1)S(1)} %fusion.26), channel_id=1, replica_groups=mesh['expert'=4,'blk'=32] {'expert'}, dimensions={1} | all-to-all | bytes 393216 | tf_op jit(solution)/shard_map/all_to_all | solution.py:28
  19.8 0.2 copy.24
  20.0 0.7 copy.40
  20.7 0.0 all-gather.3.cloned.1.call-update
  20.7 0.0 all-gather.5.cloned.1.call-start
  20.7 0.2 reduce_window_sum.18
  20.9 0.1 copy.26
  21.0 0.1 copy.27
  21.1 1.2 fusion.27
  22.3 8.7 %all_to_all.21 = bf16[1,4,128,192]{2,3,0,1:T(8,128)(2,1)S(1)} all-to-all(bf16[1,4,128,192]{2,3,0,1:T(8,128)(2,1)S(1)} %fusion.27), channel_id=1, replica_groups=mesh['expert'=4,'blk'=32] {'expert'}, dimensions={1} | all-to-all | bytes 393216 | tf_op jit(solution)/shard_map/all_to_all | solution.py:28
  31.0 0.2 copy.29
  31.1 0.7 copy.39
  31.9 0.0 all-gather.5.cloned.1.call-update
  31.9 0.0 reduce-scatter.7.cloned.1.call-start
  31.9 38.5 %all-gather.3.cloned.1.call-done = bf16[512,6144]{0,1:T(8,128)(2,1)} async-done(((bf16[512,192]{0,1:T(8,128)(2,1)}), bf16[512,6144]{0,1:T(8,128)(2,1)}) %all-gather.3.cloned.1.call-update) | async-done | bytes 6291472 | tf_op jit(solution)/shard_map/all_gather | solution.py:30
  70.5 8.2 %fusion.10 = f32[512,512]{1,0:T(8,128)S(1)} fusion(bf16[512,6144]{0,1:T(8,128)(2,1)} %all-gather.3.cloned.1.call-done, bf16[1,6144,512]{2,1,0:T(8,128)(2,1)} %param.9), kind=kOutput, calls=%fused_computation.12 | convolution fusion | flops 3221225472 | bytes 13631488 | tf_op jit(solution)/shard_map/dot_general | solution.py:31
  78.7 0.0 slice-start.1
  78.7 6.5 %fusion.21 = bf16[512,512]{1,0:T(8,128)(2,1)S(1)} fusion(bf16[512,6144]{0,1:T(8,128)(2,1)S(1)} %copy-done.1, bf16[1,6144,512]{2,1,0:T(8,128)(2,1)} %param.10, f32[512,512]{1,0:T(8,128)S(1)} %fusion.10), kind=kOutput, calls=%fused_computation.17 | convolution fusion | flops 3222798336 | bytes 14155776 | tf_op jit(solution)/shard_map/dot_general | solution.py:32
  85.2 5.3 %fusion = bf16[6144,512]{0,1:T(8,128)(2,1)} fusion(bf16[512,512]{1,0:T(8,128)(2,1)S(1)} %fusion.21, bf16[1,512,6144]{2,1,0:T(8,128)(2,1)S(1)} %bitcast.112), kind=kOutput, calls=%fused_computation.2 | convolution fusion | flops 3224371200 | bytes 13107200 | tf_op jit(solution)/shard_map/dot_general | solution.py:35
  90.5 8.7 %copy.31 = bf16[6144,512]{1,0:T(8,128)(2,1)} copy(bf16[6144,512]{0,1:T(8,128)(2,1)} %fusion) | data formatting | bytes 12582912
  99.2 0.0 reduce-scatter.7.cloned.1.call-update
  99.2 0.2 reduce-scatter.9.cloned.1.call-start
  99.4 21.5 %all-gather.5.cloned.1.call-done = bf16[512,6144]{0,1:T(8,128)(2,1)} async-done(((bf16[512,192]{0,1:T(8,128)(2,1)}), bf16[512,6144]{0,1:T(8,128)(2,1)}) %all-gather.5.cloned.1.call-update) | async-done | bytes 6291472 | tf_op jit(solution)/shard_map/all_gather | solution.py:30
  120.9 8.2 %fusion.8 = f32[512,512]{1,0:T(8,128)S(1)} fusion(bf16[512,6144]{0,1:T(8,128)(2,1)} %all-gather.5.cloned.1.call-done, bf16[1,6144,512]{2,1,0:T(8,128)(2,1)} %param.9), kind=kOutput, calls=%fused_computation.10 | convolution fusion | flops 3221225472 | bytes 13631488 | tf_op jit(solution)/shard_map/dot_general | solution.py:31
  129.1 6.5 %fusion.18 = bf16[512,512]{1,0:T(8,128)(2,1)S(1)} fusion(bf16[512,6144]{0,1:T(8,128)(2,1)S(1)} %copy-done.2, bf16[1,6144,512]{2,1,0:T(8,128)(2,1)} %param.10, f32[512,512]{1,0:T(8,128)S(1)} %fusion.8), kind=kOutput, calls=%fused_computation.16 | convolution fusion | flops 3222798336 | bytes 14155776 | tf_op jit(solution)/shard_map/dot_general | solution.py:32
  135.7 5.3 %fusion.1 = bf16[6144,512]{0,1:T(8,128)(2,1)} fusion(bf16[512,512]{1,0:T(8,128)(2,1)S(1)} %fusion.18, bf16[1,512,6144]{2,1,0:T(8,128)(2,1)S(1)} %bitcast.114), kind=kOutput, calls=%fused_computation.3 | convolution fusion | flops 3224371200 | bytes 13107200 | tf_op jit(solution)/shard_map/dot_general | solution.py:35
  141.0 8.8 %copy.33 = bf16[6144,512]{1,0:T(8,128)(2,1)} copy(bf16[6144,512]{0,1:T(8,128)(2,1)} %fusion.1) | data formatting | bytes 12582912
  149.8 0.0 reduce-scatter.9.cloned.1.call-update
  149.8 0.7 copy-done
  150.5 59.4 %reduce-scatter.7.cloned.1.call-done = bf16[192,512]{1,0:T(8,128)(2,1)} async-done(((bf16[6144,512]{1,0:T(8,128)(2,1)}), bf16[192,512]{1,0:T(8,128)(2,1)}) %reduce-scatter.7.cloned.1.call-update) | async-done | bytes 196624
  209.9 1.1 copy.32
  211.0 0.8 copy.25
  211.8 4.3 %all-to-all-start.1 = ((bf16[192,1,4,128]{3,0,1,2:T(8,128)(2,1)}), bf16[192,1,4,128]{3,0,1,2:T(8,128)(2,1)S(1)}, u32[]{:S(2)}, u32[]{:S(2)}) async-start(bf16[192,1,4,128]{3,0,1,2:T(8,128)(2,1)} %copy.25), calls=%async_computation.1 | async-start | bytes 393216 | tf_op jit(solution)/shard_map/all_to_all | solution.py:42
  216.1 83.5 %reduce-scatter.9.cloned.1.call-done = bf16[192,512]{1,0:T(8,128)(2,1)} async-done(((bf16[6144,512]{1,0:T(8,128)(2,1)}), bf16[192,512]{1,0:T(8,128)(2,1)}) %reduce-scatter.9.cloned.1.call-update) | async-done | bytes 196624
  299.6 1.1 copy.34
  300.7 0.8 copy.30
  301.5 4.3 %all-to-all-start.3 = ((bf16[192,1,4,128]{3,0,1,2:T(8,128)(2,1)}), bf16[192,1,4,128]{3,0,1,2:T(8,128)(2,1)S(1)}, u32[]{:S(2)}, u32[]{:S(2)}) async-start(bf16[192,1,4,128]{3,0,1,2:T(8,128)(2,1)} %copy.30), calls=%async_computation.3 | async-start | bytes 393216 | tf_op jit(solution)/shard_map/all_to_all | solution.py:42
  305.8 0.4 fusion.24
  306.2 5.9 %all-to-all-done.3 = bf16[192,1,4,128]{3,0,1,2:T(8,128)(2,1)S(1)} async-done(((bf16[192,1,4,128]{3,0,1,2:T(8,128)(2,1)}), bf16[192,1,4,128]{3,0,1,2:T(8,128)(2,1)S(1)}, u32[]{:S(2)}, u32[]{:S(2)}) %all-to-all-start.3) | async-done | bytes 196640 | tf_op jit(solution)/shard_map/all_to_all | solution.py:42
  312.1 0.4 fusion.25
  312.5 0.7 pad_maximum_fusion
  (22 shorter events, 0.1 us)
Async XLA Ops:
  6.5 63.9 %all-gather.3.cloned.1.call-start = ((), (), s32[]{:S(2)}) async-start(), calls=%async_computation.6 | async-start | bytes 6488064 | tf_op jit(solution)/shard_map/all_gather | solution.py:30
  20.7 100.2 %all-gather.5.cloned.1.call-start = ((), (), s32[]{:S(2)}) async-start(), calls=%async_computation.7 | async-start | bytes 6488064 | tf_op jit(solution)/shard_map/all_gather | solution.py:30
  31.9 178.0 %reduce-scatter.7.cloned.1.call-start = ((), (), s32[]{:S(2)}) async-start(), calls=%async_computation.8 | async-start | bytes 6488064
  70.5 8.2 %copy-start.1 = (bf16[512,6144]{0,1:T(8,128)(2,1)S(1)}, bf16[512,6144]{0,1:T(8,128)(2,1)}, u32[]{:S(2)}) copy-start(bf16[512,6144]{0,1:T(8,128)(2,1)} %all-gather.3.cloned.1.call-done) | copy-start | bytes 18874372
  70.5 14.7 %slice-start = ((s8[6291456]{0:T(1024)(128)(4,1)}), s8[4194304]{0:T(1024)(128)(4,1)S(1)}, s32[]{:S(2)}) async-start(s8[6291456]{0:T(1024)(128)(4,1)} %bitcast.111), calls=%async_computation.10 | async-start | bytes 8388608
  78.7 6.5 %slice-start.1 = ((s8[6291456]{0:T(1024)(128)(4,1)}), s8[2097152]{0:T(1024)(128)(4,1)S(1)}, s32[]{:S(2)}) async-start(s8[6291456]{0:T(1024)(128)(4,1)} %bitcast.111), calls=%async_computation.11 | async-start | bytes 4194304
  99.2 200.4 %reduce-scatter.9.cloned.1.call-start = ((), (), s32[]{:S(2)}) async-start(), calls=%async_computation.9 | async-start | bytes 6488064
  120.9 8.2 %copy-start.2 = (bf16[512,6144]{0,1:T(8,128)(2,1)S(1)}, bf16[512,6144]{0,1:T(8,128)(2,1)}, u32[]{:S(2)}) copy-start(bf16[512,6144]{0,1:T(8,128)(2,1)} %all-gather.5.cloned.1.call-done) | copy-start | bytes 18874372
  120.9 14.8 %slice-start.2 = ((s8[6291456]{0:T(1024)(128)(4,1)}), s8[4194304]{0:T(1024)(128)(4,1)S(1)}, s32[]{:S(2)}) async-start(s8[6291456]{0:T(1024)(128)(4,1)} %bitcast.113), calls=%async_computation.12 | async-start | bytes 8388608
  129.1 6.6 %slice-start.3 = ((s8[6291456]{0:T(1024)(128)(4,1)}), s8[2097152]{0:T(1024)(128)(4,1)S(1)}, s32[]{:S(2)}) async-start(s8[6291456]{0:T(1024)(128)(4,1)} %bitcast.113), calls=%async_computation.13 | async-start | bytes 4194304
  149.8 0.7 copy-start
  211.8 89.7 %all-to-all-start.1 = ((bf16[192,1,4,128]{3,0,1,2:T(8,128)(2,1)}), bf16[192,1,4,128]{3,0,1,2:T(8,128)(2,1)S(1)}, u32[]{:S(2)}, u32[]{:S(2)}) async-start(bf16[192,1,4,128]{3,0,1,2:T(8,128)(2,1)} %copy.25), calls=%async_computation.1 | async-start | bytes 393216 | tf_op jit(solution)/shard_map/all_to_all | solution.py:42
  301.5 10.6 %all-to-all-start.3 = ((bf16[192,1,4,128]{3,0,1,2:T(8,128)(2,1)}), bf16[192,1,4,128]{3,0,1,2:T(8,128)(2,1)S(1)}, u32[]{:S(2)}, u32[]{:S(2)}) async-start(bf16[192,1,4,128]{3,0,1,2:T(8,128)(2,1)} %copy.30), calls=%async_computation.3 | async-start | bytes 393216 | tf_op jit(solution)/shard_map/all_to_all | solution.py:42
Sparse Core Ops, SparseCore 0:
  20.8 49.6 all-gather.2
  72.7 48.1 all-gather.4
  124.6 85.2 reduce-scatter.6
  214.0 85.6 reduce-scatter.8
where the time goes:
time: 321 us; the launch traced here: 320 us
  waiting for transfers between devices  209 us (65%)
  matrix products  43.1 us (13%)
  local copies, waits for them, and re-layouts  24.7 us (8%)
  blocking collectives  19.4 us (6%)
  between operations  13.3 us (4%)
  starting transfers between devices  8.87 us (3%)
    unnamed x6, waiting for transfers between devices  143 us
    all_gather x2, waiting for transfers between devices, expert_layer(): fragment = lax.all_gather(slot_rows, 'blk', axis=1, tiled=True)  60 us
    unnamed x20, local copies, waits for them, and re-layouts  21.7 us
    all_to_all x2, blocking collectives, expert_layer(): lax.all_to_all(outgoing, 'expert', split_axis=1, concat_axis=1, tiled=True)  19.4 us
    dot_general x2, matrix products, expert_layer(): gate_pre = jnp.dot(fragment, gate_mat, preferred_element_type=jnp.float32)  16.4 us
    dot_general x2, matrix products, expert_layer(): up_pre = jnp.dot(fragment, up_mat, preferred_element_type=jnp.float32)  13.1 us
    dot_general x2, matrix products, expert_layer(): lax.dot_general(down_mat, hidden, (((0,), (1,)), ((), ())), preferred_ele...  10.6 us
    all_to_all x2, starting transfers between devices, expert_layer(): lax.all_to_all(summed.reshape(feature_cols, step_count, experts, row_coun...  8.56 us
  transfers between devices with their start and end apart: 6, of which 5 were waited for; matrix products, arithmetic and copies ran while one was open for 20% of the time, Pallas kernels for 0%

commit v1 on v0

--- a/solution.py
+++ b/solution.py
@@ -27,7 +27,9 @@
     ).astype(jnp.bfloat16)
     arrived = lax.all_to_all(outgoing, "expert", split_axis=1, concat_axis=1, tiled=True)
     slot_rows = arrived.reshape(-1, feature_cols)
-    fragment = lax.all_gather(slot_rows, "blk", axis=1, tiled=True)
+    fragment = jnp.concatenate(
+        lax.all_to_all(jnp.stack([slot_rows] * lax.axis_size("blk")), "blk", 0, 0), axis=1
+    )
     gate_pre = jnp.dot(fragment, gate_mat, preferred_element_type=jnp.float32)
     up_pre = jnp.dot(fragment, up_mat, preferred_element_type=jnp.float32)
     hidden = (jax.nn.silu(gate_pre) * up_pre).astype(jnp.bfloat16)

time: 321 us -> 370 us (1.15)
  blocking collectives: 19.4 us -> 109 us
  waiting for transfers between devices: 209 us -> 165 us
  matrix products: 43.1 us -> 35.9 us
  starting transfers between devices: 8.87 us -> 16 us
    all_to_all x0 -> x1, blocking collectives: none -> 89.7 us  [expert_layer(): lax.all_to_all(jnp.stack([slot_rows] * lax.axis_size('blk')), 'blk', 0, 0)]
    all_to_all x0 -> x1, waiting for transfers between devices: none -> 77.7 us  [expert_layer(): lax.all_to_all(jnp.stack([slot_rows] * lax.axis_size('blk')), 'blk', 0, 0)]
    unnamed x6 -> x4, waiting for transfers between devices: 143 us -> 81.2 us
    all_gather x2 -> x0, waiting for transfers between devices: 60 us -> none  [expert_layer(): fragment = lax.all_gather(slot_rows, 'blk', axis=1, tiled=True)]
    all_to_all x0 -> x1, starting transfers between devices: none -> 8.27 us  [expert_layer(): lax.all_to_all(jnp.stack([slot_rows] * lax.axis_size('blk')), 'blk', 0, 0)]
    dot_general x2, matrix products: 16.4 us -> 11.1 us  [expert_layer(): gate_pre = jnp.dot(fragment, gate_mat, preferred_element_type=jnp.float32)]
    another operation x0 -> x2, local copies, waits for them, and re-layouts: none -> 4.04 us  [expert_layer(): jnp.stack([slot_rows] * lax.axis_size('blk'))]
    unnamed x20 -> x26, local copies, waits for them, and re-layouts: 21.7 us -> 20.8 us
  transfers between devices with their start and end apart: 6 -> 5, of which waited for: 5 -> 3; matrix products, arithmetic and copies ran while one was open for 20% -> 7% of each run, Pallas kernels for 0% -> 0%
where the time goes in v1:
time: 370 us; the launch traced here: 369 us
  waiting for transfers between devices  165 us (45%)
  blocking collectives  109 us (29%)
  matrix products  35.9 us (10%)
  local copies, waits for them, and re-layouts  27.9 us (8%)
  starting transfers between devices  16 us (4%)
  between operations  13.7 us (4%)
    all_to_all x1, blocking collectives, expert_layer(): lax.all_to_all(jnp.stack([slot_rows] * lax.axis_size('blk')), 'blk', 0, 0)  89.7 us
    unnamed x4, waiting for transfers between devices  81.2 us
    all_to_all x1, waiting for transfers between devices, expert_layer(): lax.all_to_all(jnp.stack([slot_rows] * lax.axis_size('blk')), 'blk', 0, 0)  77.7 us
    unnamed x26, local copies, waits for them, and re-layouts  20.8 us
    all_to_all x2, blocking collectives, expert_layer(): lax.all_to_all(outgoing, 'expert', split_axis=1, concat_axis=1, tiled=True)  19.4 us
    dot_general x2, matrix products, expert_layer(): up_pre = jnp.dot(fragment, up_mat, preferred_element_type=jnp.float32)  11.8 us
    dot_general x2, matrix products, expert_layer(): gate_pre = jnp.dot(fragment, gate_mat, preferred_element_type=jnp.float32)  11.1 us
    dot_general x2, matrix products, expert_layer(): lax.dot_general(down_mat, hidden, (((0,), (1,)), ((), ())), preferred_ele...  10.7 us
  transfers between devices with their start and end apart: 5, of which 3 were waited for; matrix products, arithmetic and copies ran while one was open for 7% of the time, Pallas kernels for 0%

profile of v1, /device:TPU:0, one launch (start us, length us, event | category | flops | bytes accessed | tf_op | source)
XLA Modules:
  0.0 368.7 jit_solution(3311191771884708615)
XLA Ops:
  6.5 0.8 slice_bitcast_fusion.5
  7.3 0.1 fusion.45
  7.4 0.1 fusion.44
  7.6 0.2 reduce_window_sum.17
  7.8 0.1 copy.21
  7.8 0.1 copy.22
  7.9 1.2 fusion.26
  9.1 10.7 %all_to_all.30 = bf16[1,4,128,192]{2,3,0,1:T(8,128)(2,1)S(1)} all-to-all(bf16[1,4,128,192]{2,3,0,1:T(8,128)(2,1)S(1)} %fusion.26), channel_id=1, replica_groups=mesh['expert'=4,'blk'=32] {'expert'}, dimensions={1} | all-to-all | bytes 393216 | tf_op jit(solution)/shard_map/all_to_all | solution.py:28
  19.8 0.2 copy.24
  20.0 3.3 stack.6
  23.3 8.3 %all-to-all-start.1 = ((bf16[32,512,192]{1,2,0:T(8,128)(2,1)}), bf16[32,512,192]{1,2,0:T(8,128)(2,1)}, u32[]{:S(2)}, u32[]{:S(2)}) async-start(bf16[32,512,192]{1,2,0:T(8,128)(2,1)} %stack.6), calls=%async_computation.1 | async-start | bytes 12582912 | tf_op jit(solution)/shard_map/all_to_all | solution.py:31
  31.6 0.0 reduce-scatter.7.cloned.1.call-start
  31.7 0.2 reduce_window_sum.18
  31.9 77.7 %all-to-all-done.1 = bf16[32,512,192]{1,2,0:T(8,128)(2,1)} async-done(((bf16[32,512,192]{1,2,0:T(8,128)(2,1)}), bf16[32,512,192]{1,2,0:T(8,128)(2,1)}, u32[]{:S(2)}, u32[]{:S(2)}) %all-to-all-start.1) | async-done | bytes 6291488 | tf_op jit(solution)/shard_map/all_to_all | solution.py:31
  109.5 7.6 %fusion.10 = f32[512,512]{1,0:T(8,128)S(1)} fusion(bf16[512,6144]{0,1:T(8,128)(2,1)} %bitcast.10, bf16[1,6144,512]{2,1,0:T(8,128)(2,1)} %param.9), kind=kOutput, calls=%fused_computation.12 | convolution fusion | flops 3221225472 | bytes 13631488 | tf_op jit(solution)/shard_map/dot_general | solution.py:33
  117.2 0.0 slice-start.5
  117.2 8.3 %fusion.21 = bf16[512,512]{1,0:T(8,128)(2,1)S(1)} fusion(bf16[512,6144]{0,1:T(8,128)(2,1)} %bitcast.10, bf16[1,6144,512]{2,1,0:T(8,128)(2,1)} %param.10, f32[512,512]{1,0:T(8,128)S(1)} %fusion.10), kind=kOutput, calls=%fused_computation.17 | convolution fusion | flops 3222798336 | bytes 14155776 | tf_op jit(solution)/shard_map/dot_general | solution.py:34
  125.5 5.3 %fusion = bf16[6144,512]{0,1:T(8,128)(2,1)} fusion(bf16[512,512]{1,0:T(8,128)(2,1)S(1)} %fusion.21, bf16[1,512,6144]{2,1,0:T(8,128)(2,1)S(1)} %bitcast.124), kind=kOutput, calls=%fused_computation.2 | convolution fusion | flops 3224371200 | bytes 13107200 | tf_op jit(solution)/shard_map/dot_general | solution.py:37
  130.8 8.7 %copy.31 = bf16[6144,512]{1,0:T(8,128)(2,1)} copy(bf16[6144,512]{0,1:T(8,128)(2,1)} %fusion) | data formatting | bytes 12582912
  139.5 0.0 reduce-scatter.7.cloned.1.call-update
  139.5 0.0 reduce-scatter.9.cloned.1.call-start
  139.5 0.1 copy.26
  139.6 0.1 copy.27
  139.7 0.6 copy-done
  140.3 0.4 fusion.27
  140.7 8.7 %all_to_all.31 = bf16[1,4,128,192]{2,3,0,1:T(8,128)(2,1)S(1)} all-to-all(bf16[1,4,128,192]{2,3,0,1:T(8,128)(2,1)S(1)} %fusion.27), channel_id=1, replica_groups=mesh['expert'=4,'blk'=32] {'expert'}, dimensions={1} | all-to-all | bytes 393216 | tf_op jit(solution)/shard_map/all_to_all | solution.py:28
  149.4 0.2 copy.29
  149.6 0.7 stack.7
  150.3 0.0 slice-start.1
  150.4 89.7 %all_to_all.32 = bf16[32,512,192]{1,2,0:T(8,128)(2,1)S(1)} all-to-all(bf16[32,512,192]{1,2,0:T(8,128)(2,1)S(1)} %stack.7), channel_id=1, replica_groups=mesh['expert'=4,'blk'=32] {'blk'}, dimensions={0} | all-to-all | bytes 12582912 | tf_op jit(solution)/shard_map/all_to_all | solution.py:31
  240.1 3.4 fusion.8
  243.6 3.5 fusion.18
  247.2 5.4 %fusion.1 = bf16[6144,512]{0,1:T(8,128)(2,1)} fusion(bf16[512,512]{1,0:T(8,128)(2,1)S(1)} %fusion.18, bf16[1,512,6144]{2,1,0:T(8,128)(2,1)S(1)} %bitcast.126), kind=kOutput, calls=%fused_computation.3 | convolution fusion | flops 3224371200 | bytes 13107200 | tf_op jit(solution)/shard_map/dot_general | solution.py:37
  252.5 8.6 %copy.33 = bf16[6144,512]{1,0:T(8,128)(2,1)} copy(bf16[6144,512]{0,1:T(8,128)(2,1)} %fusion.1) | data formatting | bytes 12582912
  261.2 0.0 reduce-scatter.9.cloned.1.call-update
  261.2 0.7 copy-done.1
  261.9 0.0 reduce-scatter.7.cloned.1.call-done
  261.9 1.1 copy.32
  263.0 0.8 copy.25
  263.8 3.4 all-to-all-start.2
  267.2 81.1 %reduce-scatter.9.cloned.1.call-done = bf16[192,512]{1,0:T(8,128)(2,1)} async-done(((bf16[6144,512]{1,0:T(8,128)(2,1)}), bf16[192,512]{1,0:T(8,128)(2,1)}) %reduce-scatter.9.cloned.1.call-update) | async-done | bytes 196624
  348.3 1.1 copy.34
  349.4 0.8 copy.30
  350.2 4.3 %all-to-all-start.5 = ((bf16[192,1,4,128]{3,0,1,2:T(8,128)(2,1)}), bf16[192,1,4,128]{3,0,1,2:T(8,128)(2,1)S(1)}, u32[]{:S(2)}, u32[]{:S(2)}) async-start(bf16[192,1,4,128]{3,0,1,2:T(8,128)(2,1)} %copy.30), calls=%async_computation.5 | async-start | bytes 393216 | tf_op jit(solution)/shard_map/all_to_all | solution.py:44
  354.5 0.4 fusion.24
  354.9 5.9 %all-to-all-done.5 = bf16[192,1,4,128]{3,0,1,2:T(8,128)(2,1)S(1)} async-done(((bf16[192,1,4,128]{3,0,1,2:T(8,128)(2,1)}), bf16[192,1,4,128]{3,0,1,2:T(8,128)(2,1)S(1)}, u32[]{:S(2)}, u32[]{:S(2)}) %all-to-all-start.5) | async-done | bytes 196640 | tf_op jit(solution)/shard_map/all_to_all | solution.py:44
  360.8 0.4 fusion.25
  361.2 0.7 pad_maximum_fusion
  (29 shorter events, 0.1 us)
Async XLA Ops:
  23.3 86.2 %all-to-all-start.1 = ((bf16[32,512,192]{1,2,0:T(8,128)(2,1)}), bf16[32,512,192]{1,2,0:T(8,128)(2,1)}, u32[]{:S(2)}, u32[]{:S(2)}) async-start(bf16[32,512,192]{1,2,0:T(8,128)(2,1)} %stack.6), calls=%async_computation.1 | async-start | bytes 12582912 | tf_op jit(solution)/shard_map/all_to_all | solution.py:31
  31.6 230.3 %reduce-scatter.7.cloned.1.call-start = ((), (), s32[]{:S(2)}) async-start(), calls=%async_computation.8 | async-start | bytes 6488064
  109.5 15.9 %slice-start.4 = ((s8[6291456]{0:T(1024)(128)(4,1)}), s8[4194304]{0:T(1024)(128)(4,1)S(1)}, s32[]{:S(2)}) async-start(s8[6291456]{0:T(1024)(128)(4,1)} %bitcast.123), calls=%async_computation.14 | async-start | bytes 8388608
  117.2 8.3 %slice-start.5 = ((s8[6291456]{0:T(1024)(128)(4,1)}), s8[2097152]{0:T(1024)(128)(4,1)S(1)}, s32[]{:S(2)}) async-start(s8[6291456]{0:T(1024)(128)(4,1)} %bitcast.123), calls=%async_computation.15 | async-start | bytes 4194304
  139.5 0.9 copy-start
  139.5 208.8 %reduce-scatter.9.cloned.1.call-start = ((), (), s32[]{:S(2)}) async-start(), calls=%async_computation.9 | async-start | bytes 6488064
  149.6 90.5 %slice-start = ((s8[6291456]{0:T(1024)(128)(4,1)}), s8[4194304]{0:T(1024)(128)(4,1)S(1)}, s32[]{:S(2)}) async-start(s8[6291456]{0:T(1024)(128)(4,1)} %bitcast.119), calls=%async_computation.10 | async-start | bytes 8388608
  150.3 89.8 %slice-start.1 = ((s8[6291456]{0:T(1024)(128)(4,1)}), s8[2097152]{0:T(1024)(128)(4,1)S(1)}, s32[]{:S(2)}) async-start(s8[6291456]{0:T(1024)(128)(4,1)} %bitcast.119), calls=%async_computation.11 | async-start | bytes 4194304
  150.4 93.2 %slice-start.2 = ((s8[6291456]{0:T(1024)(128)(4,1)}), s8[4194304]{0:T(1024)(128)(4,1)S(1)}, s32[]{:S(2)}) async-start(s8[6291456]{0:T(1024)(128)(4,1)} %bitcast.121), calls=%async_computation.12 | async-start | bytes 8388608
  240.1 3.5 slice-start.3
  240.1 7.0 %slice-start.6 = ((s8[6291456]{0:T(1024)(128)(4,1)}), s8[4194304]{0:T(1024)(128)(4,1)S(1)}, s32[]{:S(2)}) async-start(s8[6291456]{0:T(1024)(128)(4,1)} %bitcast.125), calls=%async_computation.16 | async-start | bytes 8388608
  243.6 3.6 slice-start.7
  261.2 0.7 copy-start.1
  263.8 86.4 %all-to-all-start.2 = ((bf16[192,1,4,128]{3,0,1,2:T(8,128)(2,1)}), bf16[192,1,4,128]{3,0,1,2:T(8,128)(2,1)S(1)}, u32[]{:S(2)}, u32[]{:S(2)}) async-start(bf16[192,1,4,128]{3,0,1,2:T(8,128)(2,1)} %copy.25), calls=%async_computation.2 | async-start | bytes 393216 | tf_op jit(solution)/shard_map/all_to_all | solution.py:44
  350.2 10.6 %all-to-all-start.5 = ((bf16[192,1,4,128]{3,0,1,2:T(8,128)(2,1)}), bf16[192,1,4,128]{3,0,1,2:T(8,128)(2,1)S(1)}, u32[]{:S(2)}, u32[]{:S(2)}) async-start(bf16[192,1,4,128]{3,0,1,2:T(8,128)(2,1)} %copy.30), calls=%async_computation.5 | async-start | bytes 393216 | tf_op jit(solution)/shard_map/all_to_all | solution.py:44
Sparse Core Ops, SparseCore 0:
  139.6 118.7 reduce-scatter.6
  262.6 85.6 reduce-scatter.8
